TPU v7x, 128 devices: a whole 4x4x4 slice. The times are simulated.
128 devices in a mesh: row: 16 (over z_lo, y, core), col: 8 (over z_hi, x).
Axes of the slice: x: 4, y: 4, z: 4 (z_hi: 2, z_lo: 2; z = z_hi * 2 + z_lo), core: 2. Of those that a mesh axis runs over, the one named last changes fastest.
Arguments:
- adj_tiles: bfloat16 [16, 8, 448, 128, 128], P('row', 'col'), may hold values from -0.03125 to 0.03125
- tile_counts: int32 [16, 8, 16], P('row', 'col'), may hold values from 5 to 32, as said below
- tile_cols: int32 [16, 8, 448], P('row', 'col'), may hold values from 0 to 31, as said below
- features: bfloat16 [32768, 256], P(('col', 'row')), may hold values from -6 to 6
- weight: bfloat16 [256, 256], replicated, may hold values from -0.375 to 0.375
- upstream: bfloat16 [32768, 256], P(('row', 'col')), may hold values from -6 to 6
Outputs:
- hidden: bfloat16 [32768, 256], P(('row', 'col'))
- weight_grad: float32 [256, 256], replicated
- feature_grad: bfloat16 [32768, 256], P(('col', 'row'))
Inputs may be any that keep to these rules, and one draw needn't show every extreme that they name: `tile_counts`: entry (r, c, t) counts the nonzero tiles of row tile t in block (r, c); the counts of one block sum to 448 or less, and to exactly 448 in at least one block. `tile_cols`: live slots are filled in order of row tile; the entries of slots past a block's total count are not used.
All inputs are finite; a program needn't handle non-finite values.
Results may differ from a plain program's by a relative error of at most 0.023.
Values may be sent and summed in bfloat16 or wider, within the bound.
A program may use at most 128 MiB of HBM per device.

v0:
```python
import math

import jax
import jax.numpy as jnp
from jax import lax
from jax.sharding import PartitionSpec as P


def split_up(value, dim, length):
    before, after = (value.shape[:dim], value.shape[dim + 1 :])
    return jnp.moveaxis(value.reshape(*before, length, -1, *after), dim, 0)


def sent_and_summed(value, axis, dim):
    length = lax.axis_size(axis)
    parts = lax.all_to_all(split_up(value, dim, length), axis, 0, 0, tiled=True)
    return jnp.sum(parts.astype(jnp.float32), axis=0)


def from_everyone(value, axis):
    copies = jnp.broadcast_to(value, (lax.axis_size(axis), *value.shape))
    return lax.all_to_all(copies, axis, split_axis=0, concat_axis=0, tiled=True)


def joined_along(parts, dim):
    lengths = list(parts.shape[1:])
    lengths[dim] *= parts.shape[0]
    return jnp.moveaxis(parts, 0, dim).reshape(lengths)


def collect(value, axis, dim):
    parts = from_everyone(value, axis)
    return joined_along(parts, dim)


def slot_rows(counts, slots):
    ending = jnp.cumsum(counts)
    position = jnp.arange(slots, dtype=jnp.int32)
    return jnp.sum((position[:, None] >= ending[None, :]).astype(jnp.int32), axis=1)


def split_sum(selector, product, form):
    upper = product.astype(jnp.bfloat16)
    lower = (product - upper.astype(jnp.float32)).astype(jnp.bfloat16)
    first = jnp.einsum(form, selector, upper, preferred_element_type=jnp.float32)
    return first + jnp.einsum(form, selector, lower, preferred_element_type=jnp.float32)


def forward_block(adj_block, col_ids, counts, col_block):
    rows_t = counts.shape[0]
    group_size = adj_block.shape[0] // rows_t
    tile_size = adj_block.shape[1]
    width = col_block.shape[1]
    col_tiles = col_block.shape[0] // tile_size
    row_ids = slot_rows(counts, adj_block.shape[0])
    block_tiles = col_block.reshape(col_tiles, tile_size, width)
    col_range = jnp.arange(col_tiles, dtype=jnp.int32)
    row_range = jnp.arange(rows_t, dtype=jnp.int32)

    def forward_advance(total, pieces):
        tile_g, col_g, row_g = pieces
        pick_cols = (col_g[:, None] == col_range[None, :]).astype(jnp.bfloat16)
        picked = jnp.einsum(
            "sc,cjf->sjf", pick_cols, block_tiles, preferred_element_type=jnp.float32
        ).astype(jnp.bfloat16)
        product = jnp.einsum("sij,sjf->sif", tile_g, picked, preferred_element_type=jnp.float32)
        to_rows = (row_g[:, None] == row_range[None, :]).astype(jnp.bfloat16)
        return (total + split_sum(to_rows, product, "st,sif->tif"), None)

    stacked = (
        adj_block.reshape(rows_t, group_size, tile_size, tile_size),
        col_ids.reshape(rows_t, group_size),
        row_ids.reshape(rows_t, group_size),
    )
    total, unused = lax.scan(
        forward_advance, jnp.zeros((rows_t, tile_size, width), jnp.float32), stacked
    )
    return total.reshape(rows_t * tile_size, width)


def backward_block(adj_block, col_ids, counts, row_grad, col_tiles):
    rows_t = counts.shape[0]
    group_size = adj_block.shape[0] // rows_t
    tile_size = adj_block.shape[1]
    width = row_grad.shape[1]
    row_ids = slot_rows(counts, adj_block.shape[0])
    live = row_ids < rows_t
    targets = jnp.where(live, col_ids, col_tiles)
    grad_tiles = row_grad.reshape(rows_t, tile_size, width)
    col_range = jnp.arange(col_tiles, dtype=jnp.int32)
    row_range = jnp.arange(rows_t, dtype=jnp.int32)

    def backward_advance(total, pieces):
        tile_g, target_g, row_g = pieces
        pick_rows = (row_g[:, None] == row_range[None, :]).astype(jnp.bfloat16)
        chosen = jnp.einsum(
            "st,tif->sif", pick_rows, grad_tiles, preferred_element_type=jnp.float32
        ).astype(jnp.bfloat16)
        product = jnp.einsum("sij,sif->sjf", tile_g, chosen, preferred_element_type=jnp.float32)
        to_cols = (target_g[:, None] == col_range[None, :]).astype(jnp.bfloat16)
        return (total + split_sum(to_cols, product, "sc,sjf->cjf"), None)

    stacked = (
        adj_block.reshape(rows_t, group_size, tile_size, tile_size),
        targets.reshape(rows_t, group_size),
        row_ids.reshape(rows_t, group_size),
    )
    total, unused = lax.scan(
        backward_advance, jnp.zeros((col_tiles, tile_size, width), jnp.float32), stacked
    )
    return total.reshape(col_tiles * tile_size, width)


def activate(aggregated, weight, upstream_part):
    pre = jnp.dot(aggregated, weight, preferred_element_type=jnp.float32)
    hidden = jax.nn.silu(pre).astype(jnp.bfloat16)
    sigmoid_pre = jax.nn.sigmoid(pre)
    pre_grad = (
        upstream_part.astype(jnp.float32) * sigmoid_pre * (1.0 + pre * (1.0 - sigmoid_pre))
    ).astype(jnp.bfloat16)
    return (hidden, pre_grad)


def shards(adj_tiles, tile_counts, tile_cols, features, weight, upstream):
    adj_block = adj_tiles[0, 0]
    counts = tile_counts[0, 0]
    col_ids = tile_cols[0, 0]
    tile_size = adj_block.shape[1]
    piece_rows = upstream.shape[0]
    node_count = piece_rows * lax.axis_size("row") * lax.axis_size("col")
    col_block = lax.all_gather(features, "row", axis=0, tiled=True)
    col_tiles = col_block.shape[0] // tile_size
    partial_value = forward_block(adj_block, col_ids, counts, col_block)
    aggregated = sent_and_summed(partial_value.astype(jnp.bfloat16), "col", 0).astype(jnp.bfloat16)
    hidden, pre_grad = activate(aggregated, weight, upstream)
    local_grad = jnp.dot(aggregated.T, pre_grad, preferred_element_type=jnp.float32)
    weight_grad = lax.psum(local_grad, ("row", "col")) / math.sqrt(node_count)
    grad_piece = jnp.dot(pre_grad, weight.T, preferred_element_type=jnp.float32).astype(
        jnp.bfloat16
    )
    row_grad = collect(grad_piece, "col", 0)
    grads = backward_block(adj_block, col_ids, counts, row_grad, col_tiles)
    feature_grad = lax.psum_scatter(
        grads.astype(jnp.bfloat16), "row", scatter_dimension=0, tiled=True
    )
    return (hidden, weight_grad, feature_grad)


def solution(mesh):
    placed = (
        P("row", "col", None, None, None),
        P("row", "col", None),
        P("row", "col", None),
        P(("col", "row"), None),
        P(),
        P(("row", "col"), None),
    )
    return jax.shard_map(
        shards,
        mesh=mesh,
        in_specs=placed,
        out_specs=(P(("row", "col"), None), P(), P(("col", "row"), None)),
        check_vma=False,
    )
```

profile of v0, /device:TPU:1, one launch (start us, length us, event | category | flops | bytes accessed | tf_op | source)
XLA Modules:
  0.0 445.5 jit_solution(13702812811683327474)
XLA Ops:
  10.9 36.1 %all-gather.2.cloned.1.call-done = bf16[4096,256]{1,0:T(8,128)(2,1)} async-done(((bf16[256,256]{1,0:T(8,128)(2,1)}), bf16[4096,256]{1,0:T(8,128)(2,1)}) %all-gather.2.cloned.1.call-update) | async-done | bytes 2097168 | tf_op jit(solution)/shard_map/all_gather | solution.py:131
  47.0 4.1 copy.46
  51.1 121.3 %while.22 = (s32[]{:T(128)}, f32[16,128,256]{2,0,1:T(8,128)S(1)}, s32[16,28]{1,0:T(8,128)S(1)}, bf16[16,28,128,128]{3,2,1,0:T(8,128)(2,1)}, s32[16,28]{1,0:T(8,1...) while((s32[]{:T(128)}, f32[16,128,256]{2,0,1:T(8,128)S(1)}, ...), condition=%wide.region_3.4_spmd.clone, body=%wide.region_2.3_spmd.clone.sunk | while | flops 358483712 | bytes 22414208 | solution.py:75
  53.4 2.6 subtract_convert_fusion.4
  61.0 2.6 subtract_convert_fusion.4
  68.6 2.6 subtract_convert_fusion.4
  76.2 2.6 subtract_convert_fusion.4
  83.8 2.6 subtract_convert_fusion.4
  91.4 2.6 subtract_convert_fusion.4
  98.9 2.6 subtract_convert_fusion.4
  106.5 2.6 subtract_convert_fusion.4
  114.1 2.6 subtract_convert_fusion.4
  121.7 2.6 subtract_convert_fusion.4
  129.3 2.6 subtract_convert_fusion.4
  136.9 2.6 subtract_convert_fusion.4
  144.4 2.6 subtract_convert_fusion.4
  152.0 2.6 subtract_convert_fusion.4
  159.6 2.6 subtract_convert_fusion.4
  167.2 2.6 subtract_convert_fusion.4
  173.5 23.7 %all_to_all.10 = bf16[8,256,256]{2,1,0:T(8,128)(2,1)S(1)} all-to-all(bf16[8,256,256]{2,1,0:T(8,128)(2,1)S(1)} %bitcast.75), channel_id=1, replica_groups=mesh['row'=16,'col'=8] {'col'}, dimensions={0} | all-to-all | bytes 2097152 | tf_op jit(solution)/shard_map/all_to_all | solution.py:16
  199.6 3.6 all-to-all-start.1
  203.2 19.9 %copy.44 = bf16[1,1,448,128,128]{3,4,2,1,0:T(8,128)(2,1)} copy(bf16[1,1,448,128,128]{4,3,2,1,0:T(8,128)(2,1)} %bitcast.72) | data formatting | bytes 29360128 | tf_op args[0]
  224.9 147.6 %while.23 = (s32[]{:T(128)}, f32[32,128,256]{2,0,1:T(8,128)}, s32[16,28]{1,0:T(8,128)S(1)}, bf16[16,28,128,128]{2,3,1,0:T(8,128)(2,1)}, s32[16,28]{1,0:T(8,128)S...) while((s32[]{:T(128)}, f32[32,128,256]{2,0,1:T(8,128)}, ...), condition=%wide.region_7.8_spmd.clone, body=%wide.region_6.7_spmd.clone.sunk | while | flops 389417152 | bytes 63308724 | solution.py:108
  379.3 59.7 %reduce-scatter.2.cloned.1.call-done = bf16[256,256]{1,0:T(8,128)(2,1)} async-done(((bf16[4096,256]{1,0:T(8,128)(2,1)}), bf16[256,256]{1,0:T(8,128)(2,1)}) %reduce-scatter.2.cloned.1.call-update) | async-done | bytes 131088 | tf_op jit(solution)/shard_map/reduce_scatter | solution.py:143
  (243 shorter events, 242.3 us)
Async XLA Ops:
  7.2 190.2 %copy-start = (bf16[256,256]{1,0:T(8,128)(2,1)S(1)}, bf16[256,256]{1,0:T(8,128)(2,1)}, u32[]{:S(2)}) copy-start(bf16[256,256]{1,0:T(8,128)(2,1)} %param.14) | copy-start | bytes 393220
  7.2 39.8 %all-gather.2.cloned.1.call-start = ((), (), s32[]{:S(2)}) async-start(), calls=%async_computation.3 | async-start | bytes 2228224 | tf_op jit(solution)/shard_map/all_gather | solution.py:131
  173.5 23.8 %copy-start.4 = (bf16[256,256]{1,0:T(8,128)(2,1)S(1)}, bf16[256,256]{1,0:T(8,128)(2,1)}, u32[]{:S(2)}) copy-start(bf16[256,256]{1,0:T(8,128)(2,1)} %param.15) | copy-start | bytes 393220
  199.6 24.7 %all-to-all-start.1 = ((bf16[8,256,256]{2,1,0:T(8,128)(2,1)}), bf16[8,256,256]{2,1,0:T(8,128)(2,1)S(1)}, u32[]{:S(2)}, u32[]{:S(2)}) async-start(bf16[8,256,256]{2,1,0:T(8,128)(2,1)} %broadcast_in_dim.17), calls=%async_computation.1 | async-start | bytes 2097152 | tf_op jit(solution)/shard_map/all_to_all | solution.py:22
  203.2 174.4 %all-reduce.2.cloned.1.call-start = ((), (), s32[]{:S(2)}) async-start(), calls=%async_computation.4 | async-start | bytes 524288 | tf_op jit(solution)/shard_map/psum | solution.py:137
  224.1 214.9 %reduce-scatter.2.cloned.1.call-start = ((), (), s32[]{:S(2)}) async-start(), calls=%async_computation.5 | async-start | bytes 2228224 | tf_op jit(solution)/shard_map/reduce_scatter | solution.py:143
  228.2 2.2 copy-start.2
  237.5 2.2 copy-start.2
  246.7 2.2 copy-start.2
  255.9 2.2 copy-start.2
  259.9 2.0 copy-start.3
  265.2 2.2 copy-start.2
  274.4 2.2 copy-start.2
  283.6 2.2 copy-start.2
  292.8 2.2 copy-start.2
  302.1 2.2 copy-start.2
  311.3 2.2 copy-start.2
  320.5 2.2 copy-start.2
  329.7 2.2 copy-start.2
  338.9 2.2 copy-start.2
  348.2 2.2 copy-start.2
  357.4 2.2 copy-start.2
  366.6 2.2 copy-start.2
  375.0 63.9 %copy-start.1 = (bf16[256,256]{1,0:T(8,128)(2,1)S(1)}, bf16[256,256]{1,0:T(8,128)(2,1)}, u32[]{:S(2)}) copy-start(bf16[256,256]{1,0:T(8,128)(2,1)} %param.14) | copy-start | bytes 393220
  (15 other events, 29.4 us)
Sparse Core Ops, SparseCore 0:
  9.7 37.2 all-gather.1
  224.2 143.8 all-reduce.1
  377.7 61.2 reduce-scatter.1
where the time goes:
time: 452 us; the launch traced here: 445 us
  matrix products  222 us (49%)
  waiting for transfers between devices  96.5 us (21%)
  local copies, waits for them, and re-layouts  78 us (17%)
  blocking collectives  23.7 us (5%)
  between operations  13.9 us (3%)
  other arithmetic  5.93 us (1%)
    reduce_scatter x1, waiting for transfers between devices, shards(): lax.psum_scatter(grads.astype(jnp.bfloat16), 'row', scatter_dimension=0,...  59.7 us
    while x64, local copies, waits for them, and re-layouts  47.1 us
    dot_general x32, matrix products, split_sum(): jnp.einsum(form, selector, lower, preferred_element_type=jnp.float32)  45.8 us
    dot_general x32, matrix products, split_sum(): jnp.einsum(form, selector, upper, preferred_element_type=jnp.float32)  43.3 us
    dot_general x16, matrix products, forward_advance(): jnp.einsum('sij,sjf->sif', tile_g, picked, preferred_element_type=jnp.flo...  41 us
    dot_general x16, matrix products, backward_advance(): jnp.einsum('sij,sif->sjf', tile_g, chosen, preferred_element_type=jnp.flo...  40.8 us
    dot_general x16, matrix products, forward_advance(): jnp.einsum('sc,cjf->sjf', pick_cols, block_tiles, preferred_element_type=...  37.4 us
    all_gather x1, waiting for transfers between devices, shards(): col_block = lax.all_gather(features, 'row', axis=0, tiled=True)  36.1 us
  transfers between devices with their start and end apart: 4, of which 2 were waited for; matrix products, arithmetic and copies ran while one was open for 29% of the time, Pallas kernels for 0%

commit v1 on v0

v1 whole, which is shorter than its diff:
```python
import functools
import math

import jax
import jax.numpy as jnp
from jax import lax
from jax.experimental import pallas as pl
from jax.experimental.pallas import tpu as pltpu
from jax.sharding import PartitionSpec as P

MESH = pl.DeviceIdType.MESH
F32, BF16 = jnp.float32, jnp.bfloat16


def slot_tables(counts, cols, col_tiles):
    slots, rows_t = cols.shape[0], counts.shape[0]
    tiles = jnp.arange(rows_t, dtype=jnp.int32)
    ending = jnp.sum(jnp.where(tiles[None, :] <= tiles[:, None], counts[None, :], 0), axis=1)
    position = jnp.arange(slots, dtype=jnp.int32)
    row = jnp.sum((position[:, None] >= ending[None, :]).astype(jnp.int32), axis=1)
    key = jnp.where(row < rows_t, row * col_tiles + cols, -1 - position)
    places = jnp.arange(rows_t * col_tiles, dtype=jnp.int32)
    slot_of = jnp.min(jnp.where(key[None, :] == places[:, None], position[None, :], slots), axis=1)
    later = (key[None, :] == key[:, None]) & (position[None, :] > position[:, None])
    next_of = jnp.min(jnp.where(later, position[None, :], slots), axis=1)
    return slot_of, next_of


def layer_kernel(
    n_row, n_col, scale,
    slot_of, next_of, adj, feat, weight, upstream,
    hidden, weight_grad, feature_grad,
    a_v, x_v, send2, recv2, d_v, send_p, recv_p, acc4, send4, recv4, wl, w1, w2, w3,
    adj_sem, x_send, x_recv, xr_send, xr_recv, s2_send, s2_recv, d_send, d_recv,
    p_send, p_recv, s4_send, s4_recv, w1_send, w1_recv, w2_send, w2_recv, w3_send, w3_recv,
):
    slots = adj.shape[0]
    tile = adj.shape[1]
    piece = feat.shape[0]
    width = feat.shape[1]
    chips = n_row // 2
    col_tiles = (piece * n_row) // tile
    row = lax.axis_index("row")
    col = lax.axis_index("col")
    chip, core = row // 2, row % 2
    partner = row + 1 - 2 * core
    half_r, half_c = chips // 2, n_col // 2
    cy, cz = chip % half_r, chip // half_r
    kx, kz = col % half_c, col // half_c

    def chip_at(i):
        return ((cz + i // half_r) % 2) * half_r + (cy + i) % half_r

    def col_at(i):
        return ((kz + i // half_c) % 2) * half_c + (kx + i) % half_c

    def chip_from(i):
        return ((cz + i // half_r) % 2) * half_r + (cy + half_r - i % half_r) % half_r

    def col_from(i):
        return ((kz + i // half_c) % 2) * half_c + (kx + half_c - i % half_c) % half_c

    def rows_of(ref, r):
        return ref.at[pl.ds(pl.multiple_of(r * piece, piece), piece)]

    def remote(src, dst, send, recv, r, c):
        return pltpu.make_async_remote_copy(
            src_ref=src, dst_ref=dst, send_sem=send, recv_sem=recv, device_id=(r, c), device_id_type=MESH
        )

    adj_copy = pltpu.make_async_copy(adj, a_v.at[pl.ds(0, slots)], adj_sem)
    adj_copy.start()
    a_v[slots] = jnp.zeros((tile, tile), BF16)

    barrier = pltpu.get_barrier_semaphore()
    for i in range(1, n_row):
        pl.semaphore_signal(barrier, inc=1, device_id=((row + i) % n_row, col), device_id_type=MESH)
    for i in range(1, n_col):
        pl.semaphore_signal(barrier, inc=1, device_id=(row, (col + i) % n_col), device_id_type=MESH)
    pl.semaphore_wait(barrier, n_row + n_col - 2)

    def x_copy(i):
        return remote(feat, rows_of(x_v, row), x_send.at[i], x_recv.at[i], 2 * chip_at(i) + core, col)

    def x_relay(i, source):
        r = 2 * chip_from(i) + core
        return remote(source, rows_of(x_v, r), xr_send.at[i], xr_recv.at[i], partner, col)

    x_order = [i for i in range(1, chips)]
    for i in x_order:
        x_copy(i).start()
    x_relay(0, feat).start()
    x_v[pl.ds(pl.multiple_of(row * piece, piece), piece), :] = feat[...]

    adj_copy.wait()

    def merge(k, carry):
        s = slots - 1 - k
        a_v[s] = a_v[s] + a_v[next_of[s]]
        return carry

    lax.fori_loop(0, slots, merge, 0)

    for i in x_order:
        x_copy(i).wait_recv()
        x_relay(i, rows_of(x_v, 2 * chip_from(i) + core)).start()
    for i in range(chips):
        x_relay(i, feat).wait_recv()

    def forward(dest):
        parts = []
        for t in range(piece // tile):
            base = (dest * (piece // tile) + t) * col_tiles
            parts.append(jnp.concatenate([a_v[slot_of[base + k]] for k in range(col_tiles)], axis=1))
        return jnp.dot(jnp.concatenate(parts, axis=0), x_v[...], preferred_element_type=F32)

    def s2_copy(i):
        return remote(send2.at[i], recv2.at[i], s2_send.at[i], s2_recv.at[i], row, col_at(i))

    def forward_step(k, carry):
        i = k + 1
        send2[i] = forward(col_at(i)).astype(BF16)
        s2_copy(i).start()
        return carry

    lax.fori_loop(0, n_col - 1, forward_step, 0)
    total = forward(col)
    for i in range(1, n_col):
        s2_copy(i).wait_recv()
        total = total + recv2[i].astype(F32)
    aggregated = total.astype(BF16)

    pre = jnp.dot(aggregated, weight[...], preferred_element_type=F32)
    gate = jax.nn.sigmoid(pre)
    hidden[...] = (pre * gate).astype(BF16)
    pre_grad = (upstream[...].astype(F32) * gate * (1.0 + pre * (1.0 - gate))).astype(BF16)
    grad_t = lax.dot_general(weight[...], pre_grad, (((1,), (1,)), ((), ())), preferred_element_type=F32)
    d_v[col] = grad_t.astype(BF16)

    def d_copy(i):
        return remote(d_v.at[col], d_v.at[col], d_send.at[i], d_recv.at[i], row, col_at(i))

    for i in range(1, n_col):
        d_copy(i).start()

    agg_t = jnp.transpose(aggregated.astype(F32)).astype(BF16)
    wl[...] = jnp.dot(agg_t, pre_grad, preferred_element_type=F32).reshape(wl.shape)

    def w1_copy(i):
        r = (row + i) % n_row
        return remote(wl.at[r], w1.at[i], w1_send.at[i], w1_recv.at[i], r, col)

    def w2_copy(i):
        return remote(w2.at[col], w2.at[col], w2_send.at[i], w2_recv.at[i], row, col_at(i))

    def w3_copy(i):
        return remote(w3.at[row], w3.at[row], w3_send.at[i], w3_recv.at[i], (row + i) % n_row, col)

    for i in range(1, n_row):
        w1_copy(i).start()
    slice_sum = wl[row]
    for i in range(1, n_row):
        w1_copy(i).wait_recv()
        slice_sum = slice_sum + w1[i]
    w2[col] = slice_sum
    for i in range(1, n_col):
        w2_copy(i).start()
    for i in range(1, n_col):
        d_copy(i).wait_recv()
    for i in range(1, n_col):
        w2_copy(i).wait_recv()
    slice_sum = w2[0]
    for c in range(1, n_col):
        slice_sum = slice_sum + w2[c]
    w3[row] = slice_sum * scale
    for i in range(1, n_row):
        w3_copy(i).start()

    def backward(dest):
        acc = None
        for c in range(n_col):
            lines = []
            for t in range(piece // tile):
                base = (c * (piece // tile) + t) * col_tiles + dest * (piece // tile)
                lines.append(jnp.concatenate([a_v[slot_of[base + k]] for k in range(piece // tile)], axis=1))
            part = jnp.dot(d_v[c], jnp.concatenate(lines, axis=0), preferred_element_type=F32)
            acc = part if acc is None else acc + part
        return acc

    def p_copy(i):
        return remote(send_p.at[i], recv_p.at[i], p_send.at[i], p_recv.at[i], partner, col)

    def s4_copy(i):
        return remote(send4.at[i], recv4.at[i], s4_send.at[i], s4_recv.at[i], 2 * chip_at(i) + core, col)

    def backward_step(k, carry):
        i = (k + 1) % chips
        dest = chip_at(i)
        send_p[i] = backward(2 * dest + 1 - core).astype(BF16)
        p_copy(i).start()
        acc4[i] = backward(2 * dest + core)

        @pl.when(k > 0)
        def _():
            p_copy(k).wait_recv()
            send4[k] = (acc4[k] + recv_p[k].astype(F32)).astype(BF16)
            s4_copy(k).start()

        return carry

    lax.fori_loop(0, chips, backward_step, 0)
    p_copy(0).wait_recv()
    total = acc4[0] + recv_p[0].astype(F32)
    for i in range(1, n_row):
        w3_copy(i).wait_recv()
    weight_grad[...] = w3[...].reshape(weight_grad.shape)
    for i in range(1, chips):
        s4_copy(i).wait_recv()
        total = total + recv4[i].astype(F32)
    feature_grad[...] = jnp.transpose(total).astype(BF16)

    for i in range(1, chips):
        x_copy(i).wait_send()
        s4_copy(i).wait_send()
    for i in range(chips):
        x_relay(i, feat).wait_send()
        p_copy(i).wait_send()
    for i in range(1, n_col):
        s2_copy(i).wait_send()
        d_copy(i).wait_send()
        w2_copy(i).wait_send()
    for i in range(1, n_row):
        w1_copy(i).wait_send()
        w3_copy(i).wait_send()


def solution(mesh):
    n_row, n_col = mesh.shape["row"], mesh.shape["col"]
    chips = n_row // 2

    def shards(adj_tiles, tile_counts, tile_cols, features, weight, upstream):
        adj = adj_tiles[0, 0]
        slots, tile = adj.shape[0], adj.shape[1]
        piece, width = features.shape
        nodes = piece * n_row * n_col
        slot_of, next_of = slot_tables(tile_counts[0, 0], tile_cols[0, 0], piece * n_row // tile)
        sl = width // n_row
        dma = pltpu.SemaphoreType.DMA
        vmem = pl.BlockSpec(memory_space=pltpu.VMEM)
        smem = pl.BlockSpec(memory_space=pltpu.SMEM)
        return pl.pallas_call(
            functools.partial(layer_kernel, n_row, n_col, 1.0 / math.sqrt(nodes)),
            out_shape=(
                jax.ShapeDtypeStruct((piece, width), BF16),
                jax.ShapeDtypeStruct((width, width), F32),
                jax.ShapeDtypeStruct((piece, width), BF16),
            ),
            in_specs=[smem, smem, pl.BlockSpec(memory_space=pl.ANY), vmem, vmem, vmem],
            out_specs=(vmem, vmem, vmem),
            scratch_shapes=[
                pltpu.VMEM((slots + 1, tile, tile), BF16),
                pltpu.VMEM((piece * n_row, width), BF16),
                pltpu.VMEM((n_col, piece, width), BF16),
                pltpu.VMEM((n_col, piece, width), BF16),
                pltpu.VMEM((n_col, width, piece), BF16),
                pltpu.VMEM((chips, width, piece), BF16),
                pltpu.VMEM((chips, width, piece), BF16),
                pltpu.VMEM((chips, width, piece), F32),
                pltpu.VMEM((chips, width, piece), BF16),
                pltpu.VMEM((chips, width, piece), BF16),
                pltpu.VMEM((n_row, sl, width), F32),
                pltpu.VMEM((n_row, sl, width), F32),
                pltpu.VMEM((n_col, sl, width), F32),
                pltpu.VMEM((n_row, sl, width), F32),
                dma,
                dma((chips,)), dma((chips,)), dma((chips,)), dma((chips,)),
                dma((n_col,)), dma((n_col,)), dma((n_col,)), dma((n_col,)),
                dma((chips,)), dma((chips,)), dma((chips,)), dma((chips,)),
                dma((n_row,)), dma((n_row,)), dma((n_col,)), dma((n_col,)),
                dma((n_row,)), dma((n_row,)),
            ],
            compiler_params=pltpu.CompilerParams(
                collective_id=0, has_side_effects=True, vmem_limit_bytes=56 * 1024 * 1024
            ),
        )(slot_of, next_of, adj, features, weight, upstream)

    return jax.shard_map(
        shards,
        mesh=mesh,
        in_specs=(
            P("row", "col", None, None, None),
            P("row", "col", None),
            P("row", "col", None),
            P(("col", "row"), None),
            P(),
            P(("row", "col"), None),
        ),
        out_specs=(P(("row", "col"), None), P(), P(("col", "row"), None)),
        check_vma=False,
    )
```

time: 452 us -> 94.8 us (0.21); the launches traced: 445 us -> 94.6 us
  matrix products: 222 us -> 0 us
  waiting for transfers between devices: 96.5 us -> 0 us
  Pallas kernels: 0 us -> 85.9 us
  local copies, waits for them, and re-layouts: 78 us -> 4.8 us
  blocking collectives: 23.7 us -> 0 us
  between operations: 13.9 us -> 0.64 us
    dot_general x131 -> x0, matrix products: 222 us -> none  [the longest x32 45.8 us: split_sum(): jnp.einsum(form, selector, lower, preferred_element_type=jnp.float32)]
    pallas_call x0 -> x1, Pallas kernels: none -> 85.9 us  [shards(): pl.pallas_call(functools.partial(layer_kernel, n_row, n_col, 1.0 / math.s...]
    reduce_scatter x1 -> x0, waiting for transfers between devices: 59.7 us -> none  [shards(): lax.psum_scatter(grads.astype(jnp.bfloat16), 'row', scatter_dimension=0,...]
    while x65 -> x0, local copies, waits for them, and re-layouts: 48.2 us -> none
    all_gather x1 -> x0, waiting for transfers between devices: 36.1 us -> none  [shards(): col_block = lax.all_gather(features, 'row', axis=0, tiled=True)]
    all_to_all x1 -> x0, blocking collectives: 23.7 us -> none  [sent_and_summed(): parts = lax.all_to_all(split_up(value, dim, length), axis, 0, 0, tiled=True)]
    unnamed x10 -> x3, local copies, waits for them, and re-layouts: 25.1 us -> 4.8 us
  transfers between devices with their start and end apart: 4 -> 0, of which waited for: 2 -> 0; matrix products, arithmetic and copies ran while one was open for 29% -> 0% of each run, Pallas kernels for 0% -> 0%
where the time goes in v1:
time: 94.8 us; the launch traced here: 94.6 us
  Pallas kernels  85.9 us (91%)
  local copies, waits for them, and re-layouts  4.8 us (5%)
  other arithmetic  3.24 us (3%)
    pallas_call x1, Pallas kernels, shards(): pl.pallas_call(functools.partial(layer_kernel, n_row, n_col, 1.0 / math.s...  85.9 us
    unnamed x3, local copies, waits for them, and re-layouts  4.8 us

profile of v1, /device:TPU:1, one launch (start us, length us, event | category | flops | bytes accessed | tf_op | source)
XLA Modules:
  0.0 94.6 jit_solution(15771741217387822235)
XLA Ops:
  0.6 0.8 select_reduce_fusion.2
  1.4 0.1 convert_reduce_fusion
  1.5 0.7 subtract_select_fusion
  2.2 0.9 select_reduce_fusion.next_of
  3.1 0.8 select_reduce_fusion.1.slot_of
  3.9 85.9 %shard_map.85 = (bf16[256,256]{1,0:T(8,128)(2,1)}, f32[256,256]{1,0:T(8,128)}, bf16[256,256]{1,0:T(8,128)(2,1)}) custom-call(s32[512]{0:T(512)} %select_reduce_fusion.1.slot_of, s32[448]{0:T(512)} %select_reduce_fusion.next_of, bf16[448,128,128]{2,1,0:T(8,128)(2,1)} %bitcast.3, bf16[256,256]{1,0:T(8,128)(2,1)} %feat.1, bf16[256,256]{1,0:T(8,128)(2,1)} %weight.1, ...), custom_call_target="tpu_custom_call" | custom-call | tf_op jit(solution)/shard_map/pallas_call | solution.py:251
  89.7 1.6 %copy.12 = bf16[256,256]{1,0:T(8,128)(2,1)} copy(bf16[256,256]{1,0:T(8,128)(2,1)} %get-tuple-element.6) | data formatting | bytes 262144
  91.3 1.7 %copy.13 = f32[256,256]{1,0:T(8,128)} copy(f32[256,256]{1,0:T(8,128)} %get-tuple-element.7) | data formatting | bytes 524288
  93.0 1.6 %copy.14 = bf16[256,256]{1,0:T(8,128)(2,1)} copy(bf16[256,256]{1,0:T(8,128)(2,1)} %get-tuple-element.8) | data formatting | bytes 262144

commit v2 on v1

v2 whole, which is shorter than its diff:
```python
import functools
import math

import jax
import jax.numpy as jnp
from jax import lax
from jax.experimental import pallas as pl
from jax.experimental.pallas import tpu as pltpu
from jax.sharding import PartitionSpec as P

MESH = pl.DeviceIdType.MESH
F32, BF16 = jnp.float32, jnp.bfloat16
ADJ_CHUNKS = 8
ADJ_FIRST = 0


def slot_tables(counts, cols, col_tiles):
    slots, rows_t = cols.shape[0], counts.shape[0]
    tiles = jnp.arange(rows_t, dtype=jnp.int32)
    ending = jnp.sum(jnp.where(tiles[None, :] <= tiles[:, None], counts[None, :], 0), axis=1)
    position = jnp.arange(slots, dtype=jnp.int32)
    row = jnp.sum((position[:, None] >= ending[None, :]).astype(jnp.int32), axis=1)
    key = jnp.where(row < rows_t, row * col_tiles + cols, -1 - position)
    places = jnp.arange(rows_t * col_tiles, dtype=jnp.int32)
    slot_of = jnp.min(jnp.where(key[None, :] == places[:, None], position[None, :], slots), axis=1)
    later = (key[None, :] == key[:, None]) & (position[None, :] > position[:, None])
    next_of = jnp.min(jnp.where(later, position[None, :], slots), axis=1)
    return slot_of, next_of


def copy_kernel(*refs):
    for source, target in zip(refs[: len(refs) // 2], refs[len(refs) // 2 :]):
        target[...] = source[...]


def layer_kernel(
    n_row, n_col, scale,
    slot_of, next_of, adj, feat, weight, upstream,
    hidden, weight_grad, feature_grad,
    a_v, x_v, d_v, acc2, acc4, send2, recv2, send4, recv4, send_p, recv_p, wl, w1, w2, w3,
    adj_sem, x_send, x_recv, xr_send, xr_recv, d_send, d_recv, s2_send, s2_recv, s4_send, s4_recv,
    p_send, p_recv, w1_send, w1_recv, w2_send, w2_recv, w3_send, w3_recv,
):
    slots, tile = adj.shape[0], adj.shape[1]
    piece = feat.shape[0]
    per = piece // tile
    chips = n_row // 2
    col_tiles = per * n_row
    row = lax.axis_index("row")
    col = lax.axis_index("col")
    chip, core = row // 2, row % 2
    partner = row + 1 - 2 * core
    half_r, half_c = chips // 2, n_col // 2

    def chip_at(i):
        return ((chip // half_r + i // half_r) % 2) * half_r + (chip % half_r + i) % half_r

    def col_at(i):
        return ((col // half_c + i // half_c) % 2) * half_c + (col % half_c + i) % half_c

    def row_device(i):
        return 2 * chip_at(i) + core, col

    def col_device(i):
        return row, col_at(i)

    def remote(src, dst, send, recv, device):
        return pltpu.make_async_remote_copy(
            src_ref=src, dst_ref=dst, send_sem=send, recv_sem=recv, device_id=device, device_id_type=MESH
        )

    def gather(piece_at, device_at, half, send, recv, hook):
        moves = (
            (0, 1), (0, half - 1), (0, half),
            (0, 2),
            (half, 1), (half, half - 1),
            (2, half),
        )

        def make(h):
            up, down, plane, two, plane_up, plane_down, plane_two = [
                remote(piece_at(p, h), piece_at(p, h), send.at[7 * h + k], recv.at[7 * h + k], device_at(to))
                for k, (p, to) in enumerate(moves)
            ]

            def step(k):
                if k == 0:
                    two.start()
                    plane.start()
                    up.start()
                    down.start()
                elif k == 1:
                    up.wait_recv()
                    hook(half - 1, h)
                    down.wait_recv()
                    hook(1, h)
                elif k == 2:
                    plane.wait_recv()
                    plane_up.start()
                    plane_down.start()
                    hook(half, h)
                elif k == 3:
                    two.wait_recv()
                    plane_two.start()
                    hook(2, h)
                else:
                    plane_up.wait_recv()
                    hook(2 * half - 1, h)
                    plane_down.wait_recv()
                    hook(half + 1, h)
                    plane_two.wait_recv()
                    hook(half + 2, h)

            def finish():
                for copy in (up, down, plane, two, plane_up, plane_down, plane_two):
                    copy.wait_send()

            return step, finish

        (step0, finish0), (step1, finish1) = make(0), make(1)
        return step0, step1, lambda: (finish0(), finish1())

    def scatter(value_at, device_at, half, send_buf, recv_buf, send, recv):
        targets = (half, 1, half - 1, 1, half - 1, 2, half)
        offsets = (half + 2, half + 1, 2 * half - 1, 1, half - 1, 2, half, 0)

        def copy_of(k, h):
            n = 7 * h + k
            return remote(send_buf.at[n], recv_buf.at[n], send.at[n], recv.at[n], device_at(targets[k]))

        def got(k, h):
            copy_of(k, h).wait_recv()
            return recv_buf[7 * h + k].astype(F32)

        before = {5: (0,), 6: (1, 2), 7: (3, 4, 6, 5)}

        def step(k, h):
            value = value_at(offsets[k], h)
            for j in before.get(k, ()):
                value = value + got(j, h)
            if k < 7:
                send_buf[7 * h + k] = value.astype(BF16)
                copy_of(k, h).start()
            return value

        def finish():
            for h in range(2):
                for k in range(7):
                    copy_of(k, h).wait_send()

        return step, finish

    def packed(numbers):
        return sum(number * 8**k for k, number in enumerate(numbers))

    first_steps = ((0, 0), (1, 0), (2, 0), (3, 0), (4, 0), (0, 1), (1, 1), (2, 1))
    second_steps = ((5, 0), (6, 0), (3, 1), (4, 1), (5, 1), (6, 1), (7, 0), (7, 1))

    def run_steps(steps, half, compute, after):
        def body(n, codes):
            code, halves = codes
            compute(code % 8, halves % 8)
            for at, act in after.items():
                pl.when(n == at)(act)
            return code // 8, halves // 8

        offsets = (half + 2, half + 1, 2 * half - 1, 1, half - 1, 2, half, 0)
        lax.fori_loop(0, 8, body, (packed(offsets[k] for k, h in steps), packed(h for k, h in steps)))

    chunk = slots // ADJ_CHUNKS

    def adj_copy(k):
        part = pl.ds(k * chunk, chunk)
        return pltpu.make_async_copy(adj.at[part], a_v.at[part], adj_sem.at[k])

    for k in range(ADJ_FIRST):
        adj_copy(k).start()
    a_v[slots] = jnp.zeros((tile, tile), BF16)

    hw = feat.shape[1] // 2

    def x_piece(i, h):
        r = 2 * chip_at(i) + core
        return x_v.at[h, pl.ds(pl.multiple_of(r * piece, piece), piece)]

    for h in range(2):
        x_v[h, pl.ds(pl.multiple_of(row * piece, piece), piece), :] = feat[:, h * hw : (h + 1) * hw]

    barrier = pltpu.get_barrier_semaphore()
    for i in range(1, n_row):
        pl.semaphore_signal(barrier, inc=1, device_id=((row + i) % n_row, col), device_id_type=MESH)
    for i in range(1, n_col):
        pl.semaphore_signal(barrier, inc=1, device_id=(row, (col + i) % n_col), device_id_type=MESH)
    pl.semaphore_wait(barrier, n_row + n_col - 2)

    def x_relay(i, h):
        n = chips * h + i
        return remote(x_piece(i, h), x_piece(i, h), xr_send.at[n], xr_recv.at[n], (partner, col))

    def merge(k, carry):
        s = slots - 1 - k
        a_v[s] = a_v[s] + a_v[next_of[s]]
        return carry

    x_step0, x_step1, x_finish = gather(
        x_piece, row_device, half_r, x_send, x_recv, lambda i, h: x_relay(i, h).start()
    )
    x_step0(0)
    x_step1(0)
    x_relay(0, 0).start()
    x_relay(0, 1).start()
    for k in range(ADJ_FIRST, ADJ_CHUNKS):
        adj_copy(k).start()
    x_step0(2)
    x_step0(3)
    x_step0(1)
    x_step1(2)
    for k in range(ADJ_CHUNKS):
        adj_copy(k).wait()
    lax.fori_loop(0, slots // 2, merge, 0)
    x_step1(3)
    x_step1(1)
    lax.fori_loop(slots // 2, slots, merge, 0)
    x_step0(4)
    for i in range(chips):
        x_relay(i, 0).wait_recv()

    def forward(mine, h):
        dest = col_at(mine)
        parts = []
        for t in range(per):
            base = (dest * per + t) * col_tiles
            parts.append(jnp.concatenate([a_v[slot_of[base + k]] for k in range(col_tiles)], axis=1))
        acc2[h, mine] = jnp.dot(jnp.concatenate(parts, axis=0), x_v[h], preferred_element_type=F32)

    s2_step, s2_finish = scatter(
        lambda i, h: acc2[h, i], col_device, half_c, send2, recv2, s2_send, s2_recv
    )

    def x_end():
        for i in range(chips):
            x_relay(i, 1).wait_recv()

    def do(step, *which):
        return lambda: [step(k, h) for k, h in which] and None

    run_steps(first_steps, half_c, forward, {
        0: do(s2_step, (0, 0)),
        1: lambda: (s2_step(1, 0), x_step1(4)) and None,
        2: do(s2_step, (2, 0)),
        3: do(s2_step, (3, 0)),
        4: lambda: (s2_step(4, 0), x_end()) and None,
        5: do(s2_step, (0, 1)),
        6: do(s2_step, (1, 1)),
        7: do(s2_step, (2, 1)),
    })
    run_steps(second_steps, half_c, forward, {
        0: do(s2_step, (5, 0)),
        1: do(s2_step, (6, 0)),
        2: do(s2_step, (3, 1)),
        3: do(s2_step, (4, 1)),
        4: do(s2_step, (5, 1)),
        5: do(s2_step, (6, 1)),
    })
    aggregated = jnp.concatenate([s2_step(7, 0), s2_step(7, 1)], axis=1).astype(BF16)

    pre = jnp.dot(aggregated, weight[...], preferred_element_type=F32)
    gate = jax.nn.sigmoid(pre)
    pre_grad = (upstream[...].astype(F32) * gate * (1.0 + pre * (1.0 - gate))).astype(BF16)
    grad_t = lax.dot_general(weight[...], pre_grad, (((1,), (1,)), ((), ())), preferred_element_type=F32)
    d_v[col] = grad_t.astype(BF16)

    def w1_copy(i):
        r = (row + i) % n_row
        return remote(wl.at[r], w1.at[i], w1_send.at[i], w1_recv.at[i], (r, col))

    def w2_copy(i):
        return remote(w2.at[col], w2.at[col], w2_send.at[i], w2_recv.at[i], (row, col_at(i)))

    def w3_copy(i):
        r = 2 * chip_at(i) + core
        return remote(w3.at[row], w3.at[row], w3_send.at[i], w3_recv.at[i], (r, col))

    def w3_relay(i):
        r = 2 * chip_at((half_r - i % half_r) % half_r + half_r * (i // half_r)) + core
        return remote(w3.at[r], w3.at[r], w3_send.at[chips + i], w3_recv.at[chips + i], (partner, col))

    def sum_slices():
        total = wl[row]
        for i in range(1, n_row):
            w1_copy(i).wait_recv()
            total = total + w1[i]
        w2[col] = total
        for i in range(1, n_col):
            w2_copy(i).start()

    d_step0, d_step1, d_finish = gather(
        lambda i, h: d_v.at[col_at(i), pl.ds(h * hw, hw)], col_device, half_c, d_send, d_recv, lambda i, h: None
    )
    d_step0(0)
    d_step1(0)
    hidden[...] = (pre * gate).astype(BF16)
    agg_t = jnp.transpose(aggregated.astype(F32)).astype(BF16)
    wl[...] = jnp.dot(agg_t, pre_grad, preferred_element_type=F32).reshape(wl.shape)
    for i in range(1, n_row):
        w1_copy(i).start()
    d_step0(2)
    d_step0(3)
    d_step0(1)
    d_step1(2)
    d_step1(3)
    d_step1(1)
    sum_slices()
    d_step0(4)

    def collect_slices():
        for i in range(1, n_col):
            w2_copy(i).wait_recv()
        slice_sum = w2[0]
        for c in range(1, n_col):
            slice_sum = slice_sum + w2[c]
        w3[row] = slice_sum * scale
        for i in range(1, chips):
            w3_copy(i).start()
        w3_relay(0).start()

    def transposed_part(dest, h):
        total = None
        for c in range(n_col):
            lines = []
            for t in range(per):
                base = (c * per + t) * col_tiles + dest * per
                lines.append(jnp.concatenate([a_v[slot_of[base + k]] for k in range(per)], axis=1))
            grad = d_v[c, pl.ds(pl.multiple_of(h * hw, hw), hw), :]
            part = jnp.dot(grad, jnp.concatenate(lines, axis=0), preferred_element_type=F32)
            total = part if total is None else total + part
        return total

    def p_copy(i, h):
        n = chips * h + i
        return remote(send_p.at[n], recv_p.at[n], p_send.at[n], p_recv.at[n], (partner, col))

    def backward(mine, h):
        send_p[chips * h + mine] = transposed_part(2 * chip_at(mine) + 1 - core, h).astype(BF16)
        p_copy(mine, h).start()
        acc4[h, mine] = transposed_part(2 * chip_at(mine) + core, h)

    def joint(i, h):
        p_copy(i, h).wait_recv()
        return acc4[h, i] + recv_p[chips * h + i].astype(F32)

    s4_step, s4_finish = scatter(joint, row_device, half_r, send4, recv4, s4_send, s4_recv)
    run_steps(first_steps, half_r, backward, {
        1: do(s4_step, (0, 0)),
        2: do(s4_step, (1, 0)),
        3: lambda: (s4_step(2, 0), d_step1(4)) and None,
        4: do(s4_step, (3, 0)),
        5: do(s4_step, (4, 0)),
        6: lambda: (s4_step(0, 1), collect_slices()) and None,
        7: do(s4_step, (1, 1)),
    })
    run_steps(second_steps, half_r, backward, {
        0: do(s4_step, (2, 1)),
        1: do(s4_step, (5, 0)),
        2: do(s4_step, (6, 0)),
        3: do(s4_step, (3, 1)),
        4: do(s4_step, (4, 1)),
        5: do(s4_step, (5, 1)),
        6: do(s4_step, (6, 1)),
    })
    for i in range(1, chips):
        w3_copy(i).wait_recv()
        w3_relay(i).start()
    for i in range(chips):
        w3_relay(i).wait_recv()
    weight_grad[...] = w3[...].reshape(weight_grad.shape)
    total = jnp.concatenate([s4_step(7, 0), s4_step(7, 1)], axis=0)
    feature_grad[...] = jnp.transpose(total).astype(BF16)

    x_finish()
    d_finish()
    s2_finish()
    s4_finish()
    for i in range(chips):
        for h in range(2):
            x_relay(i, h).wait_send()
            p_copy(i, h).wait_send()
        w3_relay(i).wait_send()
    for i in range(1, chips):
        w3_copy(i).wait_send()
    for i in range(1, n_col):
        w2_copy(i).wait_send()
    for i in range(1, n_row):
        w1_copy(i).wait_send()


def solution(mesh):
    n_row, n_col = mesh.shape["row"], mesh.shape["col"]
    chips = n_row // 2

    def shards(adj_tiles, tile_counts, tile_cols, features, weight, upstream):
        adj = adj_tiles[0, 0]
        slots, tile = adj.shape[0], adj.shape[1]
        piece, width = features.shape
        nodes = piece * n_row * n_col
        slot_of, next_of = slot_tables(tile_counts[0, 0], tile_cols[0, 0], piece * n_row // tile)
        sl = width // n_row
        dma = pltpu.SemaphoreType.DMA
        vmem = pl.BlockSpec(memory_space=pltpu.VMEM)
        smem = pl.BlockSpec(memory_space=pltpu.SMEM)
        out_shape = (
            jax.ShapeDtypeStruct((piece, width), BF16),
            jax.ShapeDtypeStruct((width, width), F32),
            jax.ShapeDtypeStruct((piece, width), BF16),
        )
        results = pl.pallas_call(
            functools.partial(layer_kernel, n_row, n_col, 1.0 / math.sqrt(nodes)),
            out_shape=out_shape,
            in_specs=[smem, smem, pl.BlockSpec(memory_space=pl.ANY), vmem, vmem, vmem],
            out_specs=(vmem, vmem, vmem),
            scratch_shapes=[
                pltpu.VMEM((slots + 1, tile, tile), BF16),
                pltpu.VMEM((2, piece * n_row, width // 2), BF16),
                pltpu.VMEM((n_col, width, piece), BF16),
                pltpu.VMEM((2, 8, piece, width // 2), F32),
                pltpu.VMEM((2, 8, width // 2, piece), F32),
                pltpu.VMEM((14, piece, width // 2), BF16), pltpu.VMEM((14, piece, width // 2), BF16),
                pltpu.VMEM((14, width // 2, piece), BF16), pltpu.VMEM((14, width // 2, piece), BF16),
                pltpu.VMEM((n_row, width // 2, piece), BF16), pltpu.VMEM((n_row, width // 2, piece), BF16),
                pltpu.VMEM((n_row, sl, width), F32),
                pltpu.VMEM((n_row, sl, width), F32),
                pltpu.VMEM((n_col, sl, width), F32),
                pltpu.VMEM((n_row, sl, width), F32),
                dma((ADJ_CHUNKS,)),
                dma((14,)), dma((14,)), dma((n_row,)), dma((n_row,)),
                dma((14,)), dma((14,)), dma((14,)), dma((14,)), dma((14,)), dma((14,)),
                dma((n_row,)), dma((n_row,)),
                dma((n_row,)), dma((n_row,)), dma((n_col,)), dma((n_col,)), dma((n_row,)), dma((n_row,)),
            ],
            compiler_params=pltpu.CompilerParams(
                collective_id=0, has_side_effects=True, vmem_limit_bytes=56 * 1024 * 1024
            ),
        )(slot_of, next_of, adj, features, weight, upstream)
        return pl.pallas_call(
            copy_kernel, out_shape=out_shape, in_specs=[vmem] * 3, out_specs=(vmem,) * 3
        )(*results)

    return jax.shard_map(
        shards,
        mesh=mesh,
        in_specs=(
            P("row", "col", None, None, None),
            P("row", "col", None),
            P("row", "col", None),
            P(("col", "row"), None),
            P(),
            P(("row", "col"), None),
        ),
        out_specs=(P(("row", "col"), None), P(), P(("col", "row"), None)),
        check_vma=False,
    )
```

time: 94.8 us -> 73 us (0.77)
  Pallas kernels: 85.9 us -> 68.8 us
  local copies, waits for them, and re-layouts: 4.8 us -> 0 us
    pallas_call x1, Pallas kernels: 85.9 us -> 66.9 us  [shards(): pl.pallas_call(functools.partial(layer_kernel, n_row, n_col, 1.0 / math.s...]
    unnamed x3 -> x0, local copies, waits for them, and re-layouts: 4.8 us -> none
    pallas_call x0 -> x1, Pallas kernels: none -> 1.85 us  [shards(): pl.pallas_call(copy_kernel, out_shape=out_shape, in_specs=[vmem] * 3, out...]
where the time goes in v2:
time: 73 us; the launch traced here: 72.7 us
  Pallas kernels  68.8 us (94%)
  other arithmetic  3.24 us (4%)
    pallas_call x1, Pallas kernels, shards(): pl.pallas_call(functools.partial(layer_kernel, n_row, n_col, 1.0 / math.s...  66.9 us
    pallas_call x1, Pallas kernels, shards(): pl.pallas_call(copy_kernel, out_shape=out_shape, in_specs=[vmem] * 3, out...  1.85 us

profile of v2, /device:TPU:1, one launch (start us, length us, event | category | flops | bytes accessed | tf_op | source)
XLA Modules:
  0.0 72.7 jit_solution(11772265542240069660)
XLA Ops:
  0.6 0.8 %select_reduce_fusion.2 = s32[16]{0:T(128)S(1)} fusion(s32[16]{0:T(128)} %bitcast.5), kind=kLoop, calls=%fused_computation.7 | loop fusion | flops 752 | bytes 128 | tf_op jit(solution)/shard_map/reduce_sum | solution.py:20
  1.4 0.1 convert_reduce_fusion
  1.5 0.7 subtract_select_fusion
  2.2 0.9 %select_reduce_fusion.next_of = s32[448]{0:T(512)} fusion(s32[448]{0:T(512)S(1)} %subtract_select_fusion), kind=kLoop, calls=%fused_computation | loop fusion | flops 1003072 | bytes 3584 | tf_op jit(solution)/shard_map/reduce_min | solution.py:27
  3.1 0.8 %select_reduce_fusion.1.slot_of = s32[512]{0:T(512)} fusion(s32[448]{0:T(512)S(1)} %subtract_select_fusion), kind=kLoop, calls=%fused_computation.2 | loop fusion | flops 687616 | bytes 3840 | tf_op jit(solution)/shard_map/reduce_min | solution.py:25
  3.9 66.9 %shard_map.85 = (bf16[256,256]{1,0:T(8,128)(2,1)}, f32[256,256]{1,0:T(8,128)}, bf16[256,256]{1,0:T(8,128)(2,1)}) custom-call(s32[512]{0:T(512)} %select_reduce_fusion.1.slot_of, s32[448]{0:T(512)} %select_reduce_fusion.next_of, bf16[448,128,128]{2,1,0:T(8,128)(2,1)} %bitcast.3, bf16[256,256]{1,0:T(8,128)(2,1)} %feat.1, bf16[256,256]{1,0:T(8,128)(2,1)} %weight.1, ...), custom_call_target="tpu_custom_call" | custom-call | tf_op jit(solution)/shard_map/pallas_call | solution.py:416
  70.8 1.8 %shard_map.86 = (bf16[256,256]{1,0:T(8,128)(2,1)}, f32[256,256]{1,0:T(8,128)}, bf16[256,256]{1,0:T(8,128)(2,1)}) custom-call(bf16[256,256]{1,0:T(8,128)(2,1)} %get-tuple-element.6.refs_0_, f32[256,256]{1,0:T(8,128)} %get-tuple-element.7.refs_1_, bf16[256,256]{1,0:T(8,128)(2,1)} %get-tuple-element.8.refs_2_), custom_call_target="tpu_custom_call" | custom-call | tf_op jit(solution)/shard_map/pallas_call | solution.py:444

commit v3 on v2

--- a/solution.py
+++ b/solution.py
@@ -14,18 +14,26 @@
 ADJ_FIRST = 0
 
 
-def slot_tables(counts, cols, col_tiles):
-    slots, rows_t = cols.shape[0], counts.shape[0]
-    tiles = jnp.arange(rows_t, dtype=jnp.int32)
-    ending = jnp.sum(jnp.where(tiles[None, :] <= tiles[:, None], counts[None, :], 0), axis=1)
-    position = jnp.arange(slots, dtype=jnp.int32)
-    row = jnp.sum((position[:, None] >= ending[None, :]).astype(jnp.int32), axis=1)
-    key = jnp.where(row < rows_t, row * col_tiles + cols, -1 - position)
-    places = jnp.arange(rows_t * col_tiles, dtype=jnp.int32)
-    slot_of = jnp.min(jnp.where(key[None, :] == places[:, None], position[None, :], slots), axis=1)
-    later = (key[None, :] == key[:, None]) & (position[None, :] > position[:, None])
-    next_of = jnp.min(jnp.where(later, position[None, :], slots), axis=1)
-    return slot_of, next_of
+def table_kernel(counts, cols, slot_of, next_of):
+    rows_t, slots = counts.shape[0], cols.shape[1]
+    places = slot_of.shape[1]
+    col_tiles = places // rows_t
+    position = lax.broadcasted_iota(jnp.int32, (8, slots), 1)
+    tile_row = jnp.zeros((8, slots), jnp.int32)
+    ending = jnp.int32(0)
+    for t in range(rows_t):
+        ending = ending + counts[t]
+        tile_row = tile_row + (position >= ending).astype(jnp.int32)
+    ids = jnp.broadcast_to(cols[...], (8, slots))
+    key = jnp.where(tile_row < rows_t, tile_row * col_tiles + ids, -1 - position)
+    column = jnp.transpose(key)[:, 0:1]
+    slot = lax.broadcasted_iota(jnp.int32, (slots, places), 0)
+    place = lax.broadcasted_iota(jnp.int32, (slots, places), 1)
+    slot_of[...] = jnp.min(jnp.where(column == place, slot, slots), axis=0, keepdims=True)
+    slot = lax.broadcasted_iota(jnp.int32, (slots, slots), 0)
+    other = lax.broadcasted_iota(jnp.int32, (slots, slots), 1)
+    later = (column == key[0:1]) & (slot > other)
+    next_of[...] = jnp.min(jnp.where(later, slot, slots), axis=0, keepdims=True)
 
 
 def copy_kernel(*refs):
@@ -154,7 +162,7 @@
         return sum(number * 8**k for k, number in enumerate(numbers))
 
     first_steps = ((0, 0), (1, 0), (2, 0), (3, 0), (4, 0), (0, 1), (1, 1), (2, 1))
-    second_steps = ((5, 0), (6, 0), (3, 1), (4, 1), (5, 1), (6, 1), (7, 0), (7, 1))
+    second_steps = ((3, 1), (5, 0), (4, 1), (6, 0), (5, 1), (6, 1), (7, 0), (7, 1))
 
     def run_steps(steps, half, compute, after):
         def body(n, codes):
@@ -199,7 +207,7 @@
 
     def merge(k, carry):
         s = slots - 1 - k
-        a_v[s] = a_v[s] + a_v[next_of[s]]
+        a_v[s] = a_v[s] + a_v[next_of[0, s]]
         return carry
 
     x_step0, x_step1, x_finish = gather(
@@ -230,7 +238,7 @@
         parts = []
         for t in range(per):
             base = (dest * per + t) * col_tiles
-            parts.append(jnp.concatenate([a_v[slot_of[base + k]] for k in range(col_tiles)], axis=1))
+            parts.append(jnp.concatenate([a_v[slot_of[0, base + k]] for k in range(col_tiles)], axis=1))
         acc2[h, mine] = jnp.dot(jnp.concatenate(parts, axis=0), x_v[h], preferred_element_type=F32)
 
     s2_step, s2_finish = scatter(
@@ -255,10 +263,10 @@
         7: do(s2_step, (2, 1)),
     })
     run_steps(second_steps, half_c, forward, {
-        0: do(s2_step, (5, 0)),
-        1: do(s2_step, (6, 0)),
-        2: do(s2_step, (3, 1)),
-        3: do(s2_step, (4, 1)),
+        0: do(s2_step, (3, 1)),
+        1: do(s2_step, (5, 0)),
+        2: do(s2_step, (4, 1)),
+        3: do(s2_step, (6, 0)),
         4: do(s2_step, (5, 1)),
         5: do(s2_step, (6, 1)),
     })
@@ -330,7 +338,7 @@
             lines = []
             for t in range(per):
                 base = (c * per + t) * col_tiles + dest * per
-                lines.append(jnp.concatenate([a_v[slot_of[base + k]] for k in range(per)], axis=1))
+                lines.append(jnp.concatenate([a_v[slot_of[0, base + k]] for k in range(per)], axis=1))
             grad = d_v[c, pl.ds(pl.multiple_of(h * hw, hw), hw), :]
             part = jnp.dot(grad, jnp.concatenate(lines, axis=0), preferred_element_type=F32)
             total = part if total is None else total + part
@@ -361,10 +369,10 @@
     })
     run_steps(second_steps, half_r, backward, {
         0: do(s4_step, (2, 1)),
-        1: do(s4_step, (5, 0)),
-        2: do(s4_step, (6, 0)),
-        3: do(s4_step, (3, 1)),
-        4: do(s4_step, (4, 1)),
+        1: do(s4_step, (3, 1)),
+        2: do(s4_step, (5, 0)),
+        3: do(s4_step, (4, 1)),
+        4: do(s4_step, (6, 0)),
         5: do(s4_step, (5, 1)),
         6: do(s4_step, (6, 1)),
     })
@@ -374,8 +382,8 @@
     for i in range(chips):
         w3_relay(i).wait_recv()
     weight_grad[...] = w3[...].reshape(weight_grad.shape)
-    total = jnp.concatenate([s4_step(7, 0), s4_step(7, 1)], axis=0)
-    feature_grad[...] = jnp.transpose(total).astype(BF16)
+    for h in range(2):
+        feature_grad[:, h * hw : (h + 1) * hw] = jnp.transpose(s4_step(7, h)).astype(BF16)
 
     x_finish()
     d_finish()
@@ -403,7 +411,6 @@
         slots, tile = adj.shape[0], adj.shape[1]
         piece, width = features.shape
         nodes = piece * n_row * n_col
-        slot_of, next_of = slot_tables(tile_counts[0, 0], tile_cols[0, 0], piece * n_row // tile)
         sl = width // n_row
         dma = pltpu.SemaphoreType.DMA
         vmem = pl.BlockSpec(memory_space=pltpu.VMEM)
@@ -413,6 +420,16 @@
             jax.ShapeDtypeStruct((width, width), F32),
             jax.ShapeDtypeStruct((piece, width), BF16),
         )
+        rows_t = tile_counts.shape[2]
+        slot_of, next_of = pl.pallas_call(
+            table_kernel,
+            out_shape=(
+                jax.ShapeDtypeStruct((1, rows_t * (piece * n_row // tile)), jnp.int32),
+                jax.ShapeDtypeStruct((1, slots), jnp.int32),
+            ),
+            in_specs=[smem, vmem],
+            out_specs=(vmem, vmem),
+        )(tile_counts[0, 0], tile_cols[0])
         results = pl.pallas_call(
             functools.partial(layer_kernel, n_row, n_col, 1.0 / math.sqrt(nodes)),
             out_shape=out_shape,

time: 73 us -> 71.3 us (0.977)
  other arithmetic: 3.24 us -> 0 us
  Pallas kernels: 68.8 us -> 70.5 us
    pallas_call x0 -> x1, Pallas kernels: none -> 1.71 us  [shards(): pl.pallas_call(table_kernel, out_shape=(jax.ShapeDtypeStruct((1, rows_t *...]
    reduce_min x2 -> x0, other arithmetic: 1.69 us -> none  [the longest x1 0.91 us: slot_tables(): next_of = jnp.min(jnp.where(later, position[None, :], slots), axis=1)]
    reduce_sum x2 -> x0, other arithmetic: 0.86 us -> none  [the longest x1 0.77 us: slot_tables(): jnp.sum(jnp.where(tiles[None, :] <= tiles[:, None], counts[None, :], 0),...]
where the time goes in v3:
time: 71.3 us; the launch traced here: 71.2 us
  Pallas kernels  70.5 us (99%)
    pallas_call x1, Pallas kernels, shards(): pl.pallas_call(functools.partial(layer_kernel, n_row, n_col, 1.0 / math.s...  67 us
    pallas_call x1, Pallas kernels, shards(): pl.pallas_call(copy_kernel, out_shape=out_shape, in_specs=[vmem] * 3, out...  1.85 us
    pallas_call x1, Pallas kernels, shards(): pl.pallas_call(table_kernel, out_shape=(jax.ShapeDtypeStruct((1, rows_t *...  1.71 us

profile of v3, /device:TPU:1, one launch (start us, length us, event | category | flops | bytes accessed | tf_op | source)
XLA Modules:
  0.0 71.2 jit_solution(11988499157064761473)
XLA Ops:
  0.6 1.7 %shard_map.85 = (s32[1,512]{1,0:T(1,128)}, s32[1,448]{1,0:T(1,128)}) custom-call(s32[16]{0:T(128)} %bitcast.5, s32[1,448]{1,0:T(1,128)} %bitcast.4), custom_call_target="tpu_custom_call" | custom-call | tf_op jit(solution)/shard_map/pallas_call | solution.py:424
  2.3 67.0 %shard_map.86 = (bf16[256,256]{1,0:T(8,128)(2,1)}, f32[256,256]{1,0:T(8,128)}, bf16[256,256]{1,0:T(8,128)(2,1)}) custom-call(s32[1,512]{1,0:T(1,128)} %get-tuple-element.8.slot_of, s32[1,448]{1,0:T(1,128)} %get-tuple-element.9.next_of, bf16[448,128,128]{2,1,0:T(8,128)(2,1)} %bitcast.3, bf16[256,256]{1,0:T(8,128)(2,1)} %feat.1, bf16[256,256]{1,0:T(8,128)(2,1)} %weight.1, ...), custom_call_target="tpu_custom_call" | custom-call | tf_op jit(solution)/shard_map/pallas_call | solution.py:433
  69.3 1.8 %shard_map.87 = (bf16[256,256]{1,0:T(8,128)(2,1)}, f32[256,256]{1,0:T(8,128)}, bf16[256,256]{1,0:T(8,128)(2,1)}) custom-call(bf16[256,256]{1,0:T(8,128)(2,1)} %get-tuple-element.10.refs_0_, f32[256,256]{1,0:T(8,128)} %get-tuple-element.11.refs_1_, bf16[256,256]{1,0:T(8,128)(2,1)} %get-tuple-element.12.refs_2_), custom_call_target="tpu_custom_call" | custom-call | tf_op jit(solution)/shard_map/pallas_call | solution.py:461

commit v4 on v3

--- a/solution.py
+++ b/solution.py
@@ -59,6 +59,12 @@
     chip, core = row // 2, row % 2
     partner = row + 1 - 2 * core
     half_r, half_c = chips // 2, n_col // 2
+
+    barrier = pltpu.get_barrier_semaphore()
+    for i in range(1, n_row):
+        pl.semaphore_signal(barrier, inc=1, device_id=((row + i) % n_row, col), device_id_type=MESH)
+    for i in range(1, n_col):
+        pl.semaphore_signal(barrier, inc=1, device_id=(row, (col + i) % n_col), device_id_type=MESH)
 
     def chip_at(i):
         return ((chip // half_r + i // half_r) % 2) * half_r + (chip % half_r + i) % half_r
@@ -194,11 +200,6 @@
     for h in range(2):
         x_v[h, pl.ds(pl.multiple_of(row * piece, piece), piece), :] = feat[:, h * hw : (h + 1) * hw]
 
-    barrier = pltpu.get_barrier_semaphore()
-    for i in range(1, n_row):
-        pl.semaphore_signal(barrier, inc=1, device_id=((row + i) % n_row, col), device_id_type=MESH)
-    for i in range(1, n_col):
-        pl.semaphore_signal(barrier, inc=1, device_id=(row, (col + i) % n_col), device_id_type=MESH)
     pl.semaphore_wait(barrier, n_row + n_col - 2)
 
     def x_relay(i, h):
@@ -333,16 +334,14 @@
         w3_relay(0).start()
 
     def transposed_part(dest, h):
-        total = None
+        lines = []
         for c in range(n_col):
-            lines = []
             for t in range(per):
                 base = (c * per + t) * col_tiles + dest * per
                 lines.append(jnp.concatenate([a_v[slot_of[0, base + k]] for k in range(per)], axis=1))
-            grad = d_v[c, pl.ds(pl.multiple_of(h * hw, hw), hw), :]
-            part = jnp.dot(grad, jnp.concatenate(lines, axis=0), preferred_element_type=F32)
-            total = part if total is None else total + part
-        return total
+        rows = pl.ds(pl.multiple_of(h * hw, hw), hw)
+        grads = jnp.concatenate([d_v[c, rows, :] for c in range(n_col)], axis=1)
+        return jnp.dot(grads, jnp.concatenate(lines, axis=0), preferred_element_type=F32)
 
     def p_copy(i, h):
         n = chips * h + i

time: 71.3 us -> 71.3 us (level)
  no operation moved by 1% of the time
where the time goes in v4:
time: 71.3 us; the launch traced here: 71.1 us
  Pallas kernels  70.5 us (99%)
    pallas_call x1, Pallas kernels, shards(): pl.pallas_call(functools.partial(layer_kernel, n_row, n_col, 1.0 / math.s...  66.9 us
    pallas_call x1, Pallas kernels, shards(): pl.pallas_call(copy_kernel, out_shape=out_shape, in_specs=[vmem] * 3, out...  1.85 us
    pallas_call x1, Pallas kernels, shards(): pl.pallas_call(table_kernel, out_shape=(jax.ShapeDtypeStruct((1, rows_t *...  1.71 us

profile of v4, /device:TPU:1, one launch (start us, length us, event | category | flops | bytes accessed | tf_op | source)
XLA Modules:
  0.0 71.1 jit_solution(8537527502094289345)
XLA Ops:
  0.6 1.7 %shard_map.85 = (s32[1,512]{1,0:T(1,128)}, s32[1,448]{1,0:T(1,128)}) custom-call(s32[16]{0:T(128)} %bitcast.5, s32[1,448]{1,0:T(1,128)} %bitcast.4), custom_call_target="tpu_custom_call" | custom-call | tf_op jit(solution)/shard_map/pallas_call | solution.py:423
  2.3 66.9 %shard_map.86 = (bf16[256,256]{1,0:T(8,128)(2,1)}, f32[256,256]{1,0:T(8,128)}, bf16[256,256]{1,0:T(8,128)(2,1)}) custom-call(s32[1,512]{1,0:T(1,128)} %get-tuple-element.8.slot_of, s32[1,448]{1,0:T(1,128)} %get-tuple-element.9.next_of, bf16[448,128,128]{2,1,0:T(8,128)(2,1)} %bitcast.3, bf16[256,256]{1,0:T(8,128)(2,1)} %feat.1, bf16[256,256]{1,0:T(8,128)(2,1)} %weight.1, ...), custom_call_target="tpu_custom_call" | custom-call | tf_op jit(solution)/shard_map/pallas_call | solution.py:432
  69.3 1.8 %shard_map.87 = (bf16[256,256]{1,0:T(8,128)(2,1)}, f32[256,256]{1,0:T(8,128)}, bf16[256,256]{1,0:T(8,128)(2,1)}) custom-call(bf16[256,256]{1,0:T(8,128)(2,1)} %get-tuple-element.10.refs_0_, f32[256,256]{1,0:T(8,128)} %get-tuple-element.11.refs_1_, bf16[256,256]{1,0:T(8,128)(2,1)} %get-tuple-element.12.refs_2_), custom_call_target="tpu_custom_call" | custom-call | tf_op jit(solution)/shard_map/pallas_call | solution.py:460
